TPU v7x, 32 devices: a whole 2x2x4 slice. The times are simulated.
32 devices in a mesh: grp: 16 (over z, y, core), sub: 2 (over x).
Axes of the slice: x: 2, y: 2, z: 4, core: 2. Of those that a mesh axis runs over, the one named last changes fastest.
Arguments:
- displacement: float32 [128, 32, 256], P('grp', 'sub'), may hold values from -2 to 2
- load: float32 [128, 32, 256], P('grp', 'sub'), may hold values from -6 to 6
- kl_coef: float32 [32], replicated, may hold values from -3 to 3
- damaged: int32 [16], replicated, may hold values from 0 to 1048575, as said below
- owner: int32 [16], replicated, may hold values from 0 to 15, each once
- phase: float32 [16, 32, 1024], P('grp', 'sub'), may hold values from 1 to 10
- soften: float32 [16, 32, 1024], P('grp', 'sub'), may hold values from 0.5 to 4
Outputs:
- step_field: float32 [128, 32, 256], P('grp', 'sub')
- residual: float32 [128, 32, 256], P('grp', 'sub')
- tangents: float32 [16, 9], replicated
- point_flux: float32 [16, 3], replicated
Inputs may be any that keep to these rules, and one draw needn't show every extreme that they name: `damaged`: point p lies in rows p * 8 to (p + 1) * 8 - 1 of the first dimension, so the points are distinct cells. `owner`: each periodic cell resolves exactly one damaged point.
All inputs are finite; a program needn't handle non-finite values.
Results may differ from a plain program's by a relative error of at most 0.00045.
Values sent between devices are 32-bit elements; how exact they have to be, the bound alone decides.
A program may use at most 320 MiB of HBM per device.

v0:
```python
import jax
import jax.numpy as jnp
from jax import lax
from jax.sharding import PartitionSpec as P

M = 32
MITERS = 4
CG_ITERS = 6
K0 = 6.0
SHIFT = 0.002
HIGH = lax.Precision.HIGHEST


def extended(block, sides, width):
    for axis, dim in sides:
        count = lax.axis_size(axis)
        forward = [(i, i + 1) for i in range(count - 1)]
        backward = [(target, source) for source, target in forward]
        low = lax.ppermute(
            lax.slice_in_dim(block, block.shape[dim] - width, None, axis=dim), axis, forward
        )
        high = lax.ppermute(lax.slice_in_dim(block, 0, width, axis=dim), axis, backward)
        block = jnp.concatenate([low, block, high], axis=dim)
    return block


def passed_along(x, axis, by):
    size = lax.axis_size(axis)
    return lax.ppermute(x, axis, [(i, (i + by) % size) for i in range(size)])


def conductivity(kl_coef, xs, ys, zs, total_x, total_y, total_z):
    order = jnp.arange(4, dtype=jnp.float32)[:, None] + 1.0
    base_x = jnp.cos(jnp.pi * order * (xs.astype(jnp.float32)[None] + 0.5) / total_x)
    base_y = jnp.cos(jnp.pi * order * (ys.astype(jnp.float32)[None] + 0.5) / total_y)
    base_z = jnp.cos(jnp.pi * order[:2] * (zs.astype(jnp.float32)[None] + 0.5) / total_z)
    coef = kl_coef.reshape(2, 4, 4)
    field = jnp.einsum("cba,ai,bj,ck->ijk", coef, base_x, base_y, base_z, precision=HIGH)
    return jnp.exp(0.4 * field)


def padded_gradient(field):
    padded = extended(field, (("grp", 0), ("sub", 1)), 1)
    center = padded[:-1, :-1]
    beyond = jnp.concatenate([center[:, :, 1:], jnp.zeros_like(center[:, :, :1])], 2)
    return jnp.stack([padded[1:, :-1] - center, padded[:-1, 1:] - center, beyond - center])


def point_values(grads, flat, in_cells):
    picked = grads.reshape(3, -1)[:, flat]
    local_part = jnp.where(in_cells[None], picked, 0.0).T
    return lax.psum(local_part, ("grp", "sub"))


def divergence(grads, field, kpad, tensors, flat, target):
    flux = kpad[None] * grads
    picked = grads.reshape(3, -1)[:, flat]
    newval = jnp.einsum("pij,jp->ip", tensors, picked, precision=HIGH)
    flux = flux.reshape(3, -1).at[:, target].set(newval, mode="drop").reshape(grads.shape)
    upper_z = flux[2, 1:, 1:]
    lower_z = jnp.pad(upper_z[:, :, :-1], ((0, 0), (0, 0), (1, 0)))
    out = (
        flux[0, :-1, 1:] - flux[0, 1:, 1:] + flux[1, 1:, :-1] - flux[1, 1:, 1:] + lower_z - upper_z
    )
    return out + SHIFT * field


def along_cols(field, table, letter):
    shape = field.shape
    square = field.reshape(shape[:-1] + (M, M))
    if letter == "z":
        result = jnp.einsum("cpyz,zw->cpyw", square, table, precision=HIGH)
    else:
        result = jnp.einsum("cpyz,yw->cpwz", square, table, precision=HIGH)
    return result.reshape(shape)


def along_planes(field, table):
    return jnp.einsum("cxk,xw->cwk", field, table, precision=HIGH)


def tables_for(size):
    freq = jnp.arange(size, dtype=jnp.int32)
    angle = 2.0 * jnp.pi * (freq[:, None] * freq[None, :] % size).astype(jnp.float32) / size
    return (jnp.cos(angle), jnp.sin(angle))


def symbol_block(columns):
    freq = jnp.arange(M, dtype=jnp.int32)
    line = 4.0 * jnp.sin(jnp.pi * freq.astype(jnp.float32) / M) ** 2
    freq_y = columns // M
    freq_z = columns % M
    line_y = 4.0 * jnp.sin(jnp.pi * freq_y.astype(jnp.float32) / M) ** 2
    line_z = 4.0 * jnp.sin(jnp.pi * freq_z.astype(jnp.float32) / M) ** 2
    lam = line[:, None] + (line_y + line_z)[None, :]
    anchor = (freq[:, None] + freq_y[None, :] + freq_z[None, :] == 0).astype(jnp.float32)
    return (1.0 - anchor) / (K0 * float(M * M * M) * (lam + anchor))


def potential_solve(div, inverse, cosine, sine):
    real_part = along_cols(div, cosine, "z")
    imag_part = -along_cols(div, sine, "z")
    real_part, imag_part = (
        along_cols(real_part, cosine, "y") + along_cols(imag_part, sine, "y"),
        along_cols(imag_part, cosine, "y") - along_cols(real_part, sine, "y"),
    )
    joined = lax.all_to_all(
        jnp.stack([real_part, imag_part], 0), "sub", split_axis=3, concat_axis=2, tiled=True
    )
    real_part, imag_part = (joined[0], joined[1])
    real_part, imag_part = (
        along_planes(real_part, cosine) + along_planes(imag_part, sine),
        along_planes(imag_part, cosine) - along_planes(real_part, sine),
    )
    real_part = real_part * inverse[None]
    imag_part = imag_part * inverse[None]
    real_part, imag_part = (
        along_planes(real_part, cosine) - along_planes(imag_part, sine),
        along_planes(real_part, sine) + along_planes(imag_part, cosine),
    )
    joined = lax.all_to_all(
        jnp.stack([real_part, imag_part], 0), "sub", split_axis=2, concat_axis=3, tiled=True
    )
    real_part, imag_part = (joined[0], joined[1])
    real_part, imag_part = (
        along_cols(real_part, cosine, "y") - along_cols(imag_part, sine, "y"),
        along_cols(real_part, sine, "y") + along_cols(imag_part, cosine, "y"),
    )
    return along_cols(real_part, cosine, "z") - along_cols(imag_part, sine, "z")


def cell_strains(phi, units, last_z):
    following = passed_along(phi[:, :1], "sub", -1)
    grad_x = jnp.concatenate([phi[:, 1:], following], 1) - phi
    grad_y = jnp.roll(phi, -M, axis=2) - phi
    next_z = jnp.where(last_z, jnp.roll(phi, M - 1, axis=2), jnp.roll(phi, -1, axis=2))
    grad_z = next_z - phi
    return [units[:, i][:, None, None] + grads for i, grads in enumerate((grad_x, grad_y, grad_z))]


def micro_body(phase, soften, strain):
    planes = phase.shape[1]
    cond = phase[0] / (1.0 + soften[0] * jnp.sum(strain * strain))
    col_block = M * M // lax.axis_size("sub")
    columns = lax.axis_index("sub") * col_block + jnp.arange(col_block, dtype=jnp.int32)
    inverse = symbol_block(columns)
    cosine, sine = tables_for(M)
    units = jnp.eye(3, dtype=jnp.float32)
    col_z = jnp.arange(M * M, dtype=jnp.int32) % M
    last_z = col_z == M - 1
    first_z = col_z == 0
    phi = jnp.zeros((3, planes, M * M), jnp.float32)
    for sweep in range(MITERS):
        parts = cell_strains(phi, units, last_z)
        tau = [(cond - K0) * parts[i] for i in range(3)]
        previous = passed_along(tau[0][:, -1:], "sub", 1)
        div = tau[0] - jnp.concatenate([previous, tau[0][:, :-1]], 1)
        div = div + tau[1] - jnp.roll(tau[1], M, axis=2)
        prior_z = jnp.where(first_z, jnp.roll(tau[2], 1 - M, axis=2), jnp.roll(tau[2], 1, axis=2))
        div = div + tau[2] - prior_z
        phi = potential_solve(div, inverse, cosine, sine)
    parts = cell_strains(phi, units, last_z)
    sums = jnp.stack([jnp.sum(cond[None] * parts[i], axis=(1, 2)) for i in range(3)])
    table = lax.psum(sums, "sub") / float(M * M * M)
    return 0.5 * (table + table.T)


def residual_total(residual):
    return lax.psum(jnp.sum(residual * residual), ("grp", "sub"))


def body(displacement, load, kl_coef, damaged, owner, phase, soften):
    rows_x, rows_y, rows_z = displacement.shape
    grp_index = lax.axis_index("grp")
    sub_index = lax.axis_index("sub")
    total_x = rows_x * lax.axis_size("grp")
    total_y = rows_y * lax.axis_size("sub")
    coord_x = grp_index * rows_x - 1 + jnp.arange(rows_x + 1, dtype=jnp.int32)
    coord_y = sub_index * rows_y - 1 + jnp.arange(rows_y + 1, dtype=jnp.int32)
    coord_z = jnp.arange(rows_z, dtype=jnp.int32)
    inside = ((coord_x >= 0)[:, None, None] & (coord_y >= 0)[None, :, None]).astype(jnp.float32)
    kpad = conductivity(kl_coef, coord_x, coord_y, coord_z, total_x, total_y, rows_z) * inside
    point_z = damaged % rows_z
    rest = damaged // rows_z
    local_x = rest // total_y - grp_index * rows_x + 1
    local_y = rest % total_y - sub_index * rows_y + 1
    in_flux = (local_x >= 0) & (local_x <= rows_x) & (local_y >= 0) & (local_y <= rows_y)
    in_cells = (local_x >= 1) & (local_x <= rows_x) & (local_y >= 1) & (local_y <= rows_y)
    flat = (
        jnp.clip(local_x, 0, rows_x) * (rows_y + 1) + jnp.clip(local_y, 0, rows_y)
    ) * rows_z + point_z
    region = (rows_x + 1) * (rows_y + 1) * rows_z
    target = jnp.where(in_flux, flat, region)
    grads_u = padded_gradient(displacement)
    strains = point_values(grads_u, flat, in_cells)
    select = (owner == grp_index).astype(jnp.float32)
    rve_strain = jnp.sum(select[:, None] * strains, axis=0)
    tangent = micro_body(phase, soften, rve_strain)
    tangents = lax.all_gather(tangent.reshape(1, 9), "grp", axis=0, tiled=True)
    tensors = tangents[owner].reshape(-1, 3, 3)
    rhs = load - divergence(grads_u, displacement, kpad, tensors, flat, target)
    step_field = jnp.zeros_like(rhs)
    residual = rhs
    direction = rhs
    norm_now = residual_total(residual)
    for sweep in range(CG_ITERS):
        image = divergence(padded_gradient(direction), direction, kpad, tensors, flat, target)
        alpha = norm_now / lax.psum(jnp.sum(direction * image), ("grp", "sub"))
        step_field = step_field + alpha * direction
        residual = residual - alpha * image
        norm_next = residual_total(residual)
        direction = residual + norm_next / norm_now * direction
        norm_now = norm_next
    step_grads = point_values(padded_gradient(step_field), flat, in_cells)
    point_flux = jnp.einsum("pij,pj->pi", tensors, step_grads, precision=HIGH)
    return (step_field, residual, tangents, point_flux)


def solution(mesh):
    return jax.shard_map(
        body,
        mesh=mesh,
        in_specs=(
            P("grp", "sub", None),
            P("grp", "sub", None),
            P(),
            P(),
            P(),
            P("grp", "sub", None),
            P("grp", "sub", None),
        ),
        out_specs=(P("grp", "sub", None), P("grp", "sub", None), P(), P()),
        check_vma=False,
    )
```

profile of v0, /device:TPU:0, one launch (start us, length us, event | category | flops | bytes accessed | tf_op | source)
XLA Modules:
  0.0 2055.8 jit_solution(18226921929787480789)
XLA Ops:
  23.7 10.2 copy.503
  41.8 41.8 %psum.105 = f32[16,3]{1,0:T(8,128)S(1)} all-reduce(f32[16,3]{1,0:T(8,128)S(1)} %fusion.237), channel_id=1, replica_groups=mesh['grp'=16,'sub'=2] {'grp','sub'}, use_global_device_ids=true, to_apply=%region_0.1 | all-reduce | flops 48 | bytes 384 | tf_op jit(solution)/shard_map/psum | solution.py:52
  390.6 10.8 copy.586
  406.5 20.8 %all-gather = f32[16,1,9]{2,1,0:T(1,128)S(1)} all-gather(f32[1,1,9]{2,1,0:T(1,128)S(1)} %reshape.847), channel_id=1, replica_groups=mesh['grp'=16,'sub'=2] {'grp'}, dimensions={0}, use_global_device_ids=true | all-gather | bytes 612 | tf_op jit(solution)/shard_map/all_gather | solution.py:199
  428.3 14.0 scatter_fusion
  442.3 52.6 %fusion.696 = (f32[1,8,16,256]{0,3,2,1:T(8,128)}, f32[1,8,16,256]{0,3,2,1:T(8,128)}, f32[1,8,16,256]{0,3,2,1:T(8,128)}, f32[1,8,16,256]{0,3,2,1:T(8,128)}, f32[1,8,16,256]{0,3,2,1:T(8,128)}) fusion(f32[3,9,17,256]{0,3,2,1:T(8,128)} %bitcast.662), kind=kLoop, calls=%fused_computation.898 | loop fusion | bytes 1310720 | tf_op jit(solution)/shard_map/slice | solution.py:63
  524.8 10.0 copy.788
  560.9 10.2 copy.592
  578.6 10.2 copy.593
  588.8 14.0 scatter_fusion.1
  602.9 52.8 %fusion.695 = (f32[1,8,16,256]{0,3,2,1:T(8,128)}, f32[1,8,16,256]{0,3,2,1:T(8,128)}, f32[1,8,16,256]{0,3,2,1:T(8,128)}, f32[1,8,16,256]{0,3,2,1:T(8,128)}, f32[1,8,16,256]{0,3,2,1:T(8,128)}) fusion(f32[3,9,17,256]{0,3,2,1:T(8,128)} %bitcast.664), kind=kLoop, calls=%fused_computation.897 | loop fusion | bytes 1310720 | tf_op jit(solution)/shard_map/slice | solution.py:63
  665.6 9.9 copy.795
  695.4 9.9 copy.791
  706.1 39.2 %all-reduce.19 = (f32[]{:T(128)}, f32[]{:T(128)}) all-reduce(f32[]{:T(128)} %get-tuple-element.8, f32[]{:T(128)} %get-tuple-element.7), channel_id=1, replica_groups=mesh['grp'=16,'sub'=2] {'grp','sub'}, use_global_device_ids=true, to_apply=%region_9.10 | all-reduce | flops 2 | bytes 16 | tf_op jit(solution)/shard_map/psum | solution.py:169
  747.3 40.9 %psum.109 = f32[]{:T(128)} all-reduce(f32[]{:T(128)} %multiply_reduce_fusion.11), channel_id=1, replica_groups=mesh['grp'=16,'sub'=2] {'grp','sub'}, use_global_device_ids=true, to_apply=%region_14.15 | all-reduce | flops 1 | bytes 8 | tf_op jit(solution)/shard_map/psum | solution.py:169
  805.5 10.2 copy.599
  823.3 10.2 copy.600
  833.5 14.0 scatter_fusion.2
  847.6 52.8 %fusion.694 = (f32[1,8,16,256]{0,3,2,1:T(8,128)}, f32[1,8,16,256]{0,3,2,1:T(8,128)}, f32[1,8,16,256]{0,3,2,1:T(8,128)}, f32[1,8,16,256]{0,3,2,1:T(8,128)}, f32[1,8,16,256]{0,3,2,1:T(8,128)}) fusion(f32[3,9,17,256]{0,3,2,1:T(8,128)} %bitcast.665), kind=kLoop, calls=%fused_computation.896 | loop fusion | bytes 1310720 | tf_op jit(solution)/shard_map/slice | solution.py:63
  930.2 9.9 copy.798
  950.8 40.7 %psum.110 = f32[]{:T(128)} all-reduce(f32[]{:T(128)} %get-tuple-element.27), channel_id=1, replica_groups=mesh['grp'=16,'sub'=2] {'grp','sub'}, use_global_device_ids=true, to_apply=%region_17.18 | all-reduce | flops 1 | bytes 8 | tf_op jit(solution)/shard_map/psum | solution.py:208
  993.5 40.1 %psum.111 = f32[]{:T(128)} all-reduce(f32[]{:T(128)} %get-tuple-element.25), channel_id=1, replica_groups=mesh['grp'=16,'sub'=2] {'grp','sub'}, use_global_device_ids=true, to_apply=%region_19.20 | all-reduce | flops 1 | bytes 8 | tf_op jit(solution)/shard_map/psum | solution.py:169
  1052.3 10.2 copy.606
  1070.0 10.2 copy.607
  1080.2 14.0 scatter_fusion.3
  1094.3 53.1 %fusion.693 = (f32[1,8,16,256]{0,3,2,1:T(8,128)}, f32[1,8,16,256]{0,3,2,1:T(8,128)}, f32[1,8,16,256]{0,3,2,1:T(8,128)}, f32[1,8,16,256]{0,3,2,1:T(8,128)}, f32[1,8,16,256]{0,3,2,1:T(8,128)}) fusion(f32[3,9,17,256]{0,3,2,1:T(8,128)} %bitcast.666), kind=kLoop, calls=%fused_computation.895 | loop fusion | bytes 1310720 | tf_op jit(solution)/shard_map/slice | solution.py:63
  1197.8 40.4 %psum.112 = f32[]{:T(128)} all-reduce(f32[]{:T(128)} %get-tuple-element.23), channel_id=1, replica_groups=mesh['grp'=16,'sub'=2] {'grp','sub'}, use_global_device_ids=true, to_apply=%region_22.23 | all-reduce | flops 1 | bytes 8 | tf_op jit(solution)/shard_map/psum | solution.py:208
  1240.1 40.2 %psum.113 = f32[]{:T(128)} all-reduce(f32[]{:T(128)} %get-tuple-element.21), channel_id=1, replica_groups=mesh['grp'=16,'sub'=2] {'grp','sub'}, use_global_device_ids=true, to_apply=%region_24.25 | all-reduce | flops 1 | bytes 8 | tf_op jit(solution)/shard_map/psum | solution.py:169
  1298.3 10.2 copy.613
  1316.0 10.2 copy.614
  1326.3 14.0 scatter_fusion.4
  1340.3 52.8 %fusion.692 = (f32[1,8,16,256]{0,3,2,1:T(8,128)}, f32[1,8,16,256]{0,3,2,1:T(8,128)}, f32[1,8,16,256]{0,3,2,1:T(8,128)}, f32[1,8,16,256]{0,3,2,1:T(8,128)}, f32[1,8,16,256]{0,3,2,1:T(8,128)}) fusion(f32[3,9,17,256]{0,3,2,1:T(8,128)} %bitcast.667), kind=kLoop, calls=%fused_computation.894 | loop fusion | bytes 1310720 | tf_op jit(solution)/shard_map/slice | solution.py:63
  1443.5 40.7 %psum.114 = f32[]{:T(128)} all-reduce(f32[]{:T(128)} %get-tuple-element.19), channel_id=1, replica_groups=mesh['grp'=16,'sub'=2] {'grp','sub'}, use_global_device_ids=true, to_apply=%region_27.28 | all-reduce | flops 1 | bytes 8 | tf_op jit(solution)/shard_map/psum | solution.py:208
  1486.2 39.9 %psum.115 = f32[]{:T(128)} all-reduce(f32[]{:T(128)} %get-tuple-element.17), channel_id=1, replica_groups=mesh['grp'=16,'sub'=2] {'grp','sub'}, use_global_device_ids=true, to_apply=%region_29.30 | all-reduce | flops 1 | bytes 8 | tf_op jit(solution)/shard_map/psum | solution.py:169
  1545.0 10.2 copy.620
  1562.7 10.2 copy.621
  1572.9 14.0 scatter_fusion.5
  1587.0 52.8 %fusion.691 = (f32[1,8,16,256]{0,3,2,1:T(8,128)}, f32[1,8,16,256]{0,3,2,1:T(8,128)}, f32[1,8,16,256]{0,3,2,1:T(8,128)}, f32[1,8,16,256]{0,3,2,1:T(8,128)}, f32[1,8,16,256]{0,3,2,1:T(8,128)}) fusion(f32[3,9,17,256]{0,3,2,1:T(8,128)} %bitcast.668), kind=kLoop, calls=%fused_computation.893 | loop fusion | bytes 1310720 | tf_op jit(solution)/shard_map/slice | solution.py:63
  1690.2 40.4 %psum.116 = f32[]{:T(128)} all-reduce(f32[]{:T(128)} %get-tuple-element.15), channel_id=1, replica_groups=mesh['grp'=16,'sub'=2] {'grp','sub'}, use_global_device_ids=true, to_apply=%region_32.33 | all-reduce | flops 1 | bytes 8 | tf_op jit(solution)/shard_map/psum | solution.py:208
  1732.6 40.2 %psum.117 = f32[]{:T(128)} all-reduce(f32[]{:T(128)} %get-tuple-element.13), channel_id=1, replica_groups=mesh['grp'=16,'sub'=2] {'grp','sub'}, use_global_device_ids=true, to_apply=%region_34.35 | all-reduce | flops 1 | bytes 8 | tf_op jit(solution)/shard_map/psum | solution.py:169
  1790.8 10.2 copy.627
  1808.5 10.2 copy.628
  1818.8 14.0 scatter_fusion.6
  1832.8 52.8 %fusion.690 = (f32[1,8,16,256]{0,3,2,1:T(8,128)}, f32[1,8,16,256]{0,3,2,1:T(8,128)}, f32[1,8,16,256]{0,3,2,1:T(8,128)}, f32[1,8,16,256]{0,3,2,1:T(8,128)}, f32[1,8,16,256]{0,3,2,1:T(8,128)}) fusion(f32[3,9,17,256]{0,3,2,1:T(8,128)} %bitcast.663), kind=kLoop, calls=%fused_computation.892 | loop fusion | bytes 1310720 | tf_op jit(solution)/shard_map/slice | solution.py:63
  1915.5 10.0 copy.818
  1936.2 40.6 %psum.118 = f32[]{:T(128)} all-reduce(f32[]{:T(128)} %get-tuple-element.11), channel_id=1, replica_groups=mesh['grp'=16,'sub'=2] {'grp','sub'}, use_global_device_ids=true, to_apply=%region_37.38 | all-reduce | flops 1 | bytes 8 | tf_op jit(solution)/shard_map/psum | solution.py:208
  1995.3 10.2 copy.634
  2012.9 41.3 %psum.119 = f32[16,3]{1,0:T(8,128)S(1)} all-reduce(f32[16,3]{1,0:T(8,128)S(1)} %broadcast_select_fusion), channel_id=1, replica_groups=mesh['grp'=16,'sub'=2] {'grp','sub'}, use_global_device_ids=true, to_apply=%region_38.39 | all-reduce | flops 48 | bytes 384 | tf_op jit(solution)/shard_map/psum | solution.py:52
  (615 shorter events, 818.4 us)
Async XLA Ops:
  0.7 84.9 %collective-permute-start.4 = (f32[3,1,1024]{2,1,0:T(1,128)S(1)}, f32[3,1,1024]{2,1,0:T(1,128)S(1)}, u32[]{:S(2)}, u32[]{:S(2)}) collective-permute-start(f32[3,1,1024]{2,1,0:T(1,128)S(1)} %slice.710), channel_id=1, source_target_pairs={{0,1},{1,0},{2,3},{3,2},{4,5},{5,4},{6,7},{7,6},{8,9},{9,8},{10,11... | collective-permute-start | bytes 36872 | tf_op jit(solution)/shard_map/ppermute | solution.py:29
  4.4 10.0 collective-permute-start.1
  5.7 7.7 collective-permute-start
  14.5 6.0 collective-permute-start.3
  15.8 5.9 collective-permute-start.2
  86.4 4.0 collective-permute-start.5
  106.7 9.5 all-to-all-start
  147.8 3.8 collective-permute-start.6
  154.1 10.8 collective-permute-start.7
  227.2 3.8 collective-permute-start.8
  233.4 10.1 collective-permute-start.9
  306.0 3.8 collective-permute-start.10
  312.2 9.4 collective-permute-start.11
  341.7 9.3 all-to-all-start.6
  368.3 9.3 all-to-all-start.7
  384.8 3.8 collective-permute-start.12
  544.9 448.0 %copy-start = (f32[8,16,256]{2,1,0:T(8,128)}, f32[8,16,256]{2,1,0:T(8,128)S(1)}, u32[]{:S(2)}) copy-start(f32[8,16,256]{2,1,0:T(8,128)S(1)} %fusion.102) | copy-start | bytes 393220
  544.9 3.6 collective-permute-start.13
  547.1 3.1 collective-permute-start.14
  550.2 5.3 collective-permute-start.15
  554.2 5.6 collective-permute-start.16
  789.6 245.3 %copy-start.4 = (f32[8,16,256]{2,1,0:T(8,128)}, f32[8,16,256]{2,1,0:T(8,128)S(1)}, u32[]{:S(2)}) copy-start(f32[8,16,256]{2,1,0:T(8,128)S(1)} %multiply_add_fusion.5) | copy-start | bytes 393220
  789.6 2.6 collective-permute-start.17
  790.9 5.8 collective-permute-start.18
  796.7 3.5 collective-permute-start.19
  798.8 5.6 collective-permute-start.20
  1034.9 246.7 %copy-start.6 = (f32[8,16,256]{2,1,0:T(8,128)}, f32[8,16,256]{2,1,0:T(8,128)S(1)}, u32[]{:S(2)}) copy-start(f32[8,16,256]{2,1,0:T(8,128)S(1)} %multiply_add_fusion.4) | copy-start | bytes 393220
  1034.9 2.6 collective-permute-start.21
  1036.2 5.8 collective-permute-start.22
  1042.0 4.9 collective-permute-start.23
  1045.6 5.6 collective-permute-start.24
  1281.7 245.7 %copy-start.8 = (f32[8,16,256]{2,1,0:T(8,128)}, f32[8,16,256]{2,1,0:T(8,128)S(1)}, u32[]{:S(2)}) copy-start(f32[8,16,256]{2,1,0:T(8,128)S(1)} %multiply_add_fusion.3) | copy-start | bytes 393220
  1281.7 2.6 collective-permute-start.25
  1283.0 5.8 collective-permute-start.26
  1288.8 4.2 collective-permute-start.27
  1291.6 5.6 collective-permute-start.28
  1527.5 2.6 collective-permute-start.29
  1528.8 5.8 collective-permute-start.30
  1534.6 5.1 collective-permute-start.31
  1538.3 5.6 collective-permute-start.32
  1774.1 2.6 collective-permute-start.33
  1775.4 5.8 collective-permute-start.34
  1781.2 4.3 collective-permute-start.35
  1784.1 5.6 collective-permute-start.36
  1978.3 2.6 collective-permute-start.37
  1979.6 5.8 collective-permute-start.38
  1985.4 4.7 collective-permute-start.39
  1988.8 5.6 collective-permute-start.40
  (31 other events, 1716.0 us)
where the time goes:
time: 2070 us; the launch traced here: 2060 us
  local copies, waits for them, and re-layouts  1160 us (56%)
  blocking collectives  596 us (29%)
  waiting for transfers between devices  82.4 us (4%)
  starting transfers between devices  76.9 us (4%)
  matrix products  60.3 us (3%)
  other arithmetic  57.4 us (3%)
    unnamed x118, local copies, waits for them, and re-layouts  392 us
    slice x7, local copies, waits for them, and re-layouts, divergence(): flux[0, 1:, 1:]  370 us
    psum x6, blocking collectives, residual_total(): return lax.psum(jnp.sum(residual * residual), ('grp', 'sub'))  240 us
    psum x5, blocking collectives, body(): alpha = norm_now / lax.psum(jnp.sum(direction * image), ('grp', 'sub'))  203 us
    scatter x7, local copies, waits for them, and re-layouts, divergence(): flux.reshape(3, -1).at[:, target].set(newval, mode='drop')  98.3 us
    another operation x32, local copies, waits for them, and re-layouts, padded_gradient(): jnp.stack([padded[1:, :-1] - center, padded[:-1, 1:] - center, beyond - c...  85.6 us
    psum x2, blocking collectives, point_values(): return lax.psum(local_part, ('grp', 'sub'))  83.1 us
    mul x8, local copies, waits for them, and re-layouts, divergence(): flux = kpad[None] * grads  72.2 us
  transfers between devices with their start and end apart: 44, of which 28 were waited for; matrix products, arithmetic and copies ran while one was open for 3% of the time, Pallas kernels for 0%

commit v1 on v0

--- a/solution.py
+++ b/solution.py
@@ -9,6 +9,15 @@
 K0 = 6.0
 SHIFT = 0.002
 HIGH = lax.Precision.HIGHEST
+cover_state = lambda panel: jnp.concatenate(
+    jax.lax.all_to_all(
+        jnp.stack(jnp.split(panel, jax.lax.axis_size("sub"), axis=3), axis=0),
+        axis_name="sub",
+        split_axis=0,
+        concat_axis=0,
+    ),
+    axis=2,
+)
 
 
 def extended(block, sides, width):
@@ -104,9 +113,7 @@
         along_cols(real_part, cosine, "y") + along_cols(imag_part, sine, "y"),
         along_cols(imag_part, cosine, "y") - along_cols(real_part, sine, "y"),
     )
-    joined = lax.all_to_all(
-        jnp.stack([real_part, imag_part], 0), "sub", split_axis=3, concat_axis=2, tiled=True
-    )
+    joined = cover_state(jnp.stack([real_part, imag_part], 0))
     real_part, imag_part = (joined[0], joined[1])
     real_part, imag_part = (
         along_planes(real_part, cosine) + along_planes(imag_part, sine),

time: 2070 us -> 1980 us (0.957)
  local copies, waits for them, and re-layouts: 1160 us -> 1090 us
    unnamed x118 -> x116, local copies, waits for them, and re-layouts: 392 us -> 350 us
where the time goes in v1:
time: 1980 us; the launch traced here: 1970 us
  local copies, waits for them, and re-layouts  1090 us (55%)
  blocking collectives  596 us (30%)
  waiting for transfers between devices  84.8 us (4%)
  starting transfers between devices  76.9 us (4%)
  matrix products  60.1 us (3%)
  other arithmetic  44 us (2%)
    slice x7, local copies, waits for them, and re-layouts, divergence(): flux[0, 1:, 1:]  370 us
    unnamed x116, local copies, waits for them, and re-layouts  350 us
    psum x6, blocking collectives, residual_total(): return lax.psum(jnp.sum(residual * residual), ('grp', 'sub'))  240 us
    psum x5, blocking collectives, body(): alpha = norm_now / lax.psum(jnp.sum(direction * image), ('grp', 'sub'))  203 us
    scatter x7, local copies, waits for them, and re-layouts, divergence(): flux.reshape(3, -1).at[:, target].set(newval, mode='drop')  99.8 us
    another operation x32, local copies, waits for them, and re-layouts, padded_gradient(): jnp.stack([padded[1:, :-1] - center, padded[:-1, 1:] - center, beyond - c...  85.4 us
    psum x2, blocking collectives, point_values(): return lax.psum(local_part, ('grp', 'sub'))  82.6 us
    mul x8, local copies, waits for them, and re-layouts, divergence(): flux = kpad[None] * grads  71.8 us
  transfers between devices with their start and end apart: 44, of which 28 were waited for; matrix products, arithmetic and copies ran while one was open for 3% of the time, Pallas kernels for 0%

profile of v1, /device:TPU:0, one launch (start us, length us, event | category | flops | bytes accessed | tf_op | source)
XLA Modules:
  0.0 1966.8 jit_solution(13915189382305955545)
XLA Ops:
  23.7 10.1 copy.507
  41.2 41.3 %psum.105 = f32[16,3]{1,0:T(8,128)S(1)} all-reduce(f32[16,3]{1,0:T(8,128)S(1)} %fusion.237), channel_id=1, replica_groups=mesh['grp'=16,'sub'=2] {'grp','sub'}, use_global_device_ids=true, to_apply=%region_0.1 | all-reduce | flops 48 | bytes 384 | tf_op jit(solution)/shard_map/psum | solution.py:61
  205.3 10.7 all_to_all.83
  300.7 10.6 copy.590
  316.4 20.5 %all-gather = f32[16,1,9]{2,1,0:T(1,128)S(1)} all-gather(f32[1,1,9]{2,1,0:T(1,128)S(1)} %reshape.867), channel_id=1, replica_groups=mesh['grp'=16,'sub'=2] {'grp'}, dimensions={0}, use_global_device_ids=true | all-gather | bytes 612 | tf_op jit(solution)/shard_map/all_gather | solution.py:206
  338.0 14.2 scatter_fusion
  352.1 52.8 %fusion.696 = (f32[1,8,16,256]{0,3,2,1:T(8,128)}, f32[1,8,16,256]{0,3,2,1:T(8,128)}, f32[1,8,16,256]{0,3,2,1:T(8,128)}, f32[1,8,16,256]{0,3,2,1:T(8,128)}, f32[1,8,16,256]{0,3,2,1:T(8,128)}) fusion(f32[3,9,17,256]{0,3,2,1:T(8,128)} %bitcast.666), kind=kLoop, calls=%fused_computation.914 | loop fusion | bytes 1310720 | tf_op jit(solution)/shard_map/slice | solution.py:72
  424.8 9.9 copy.793
  434.8 10.0 copy.792
  444.8 9.9 copy.790
  470.9 10.2 copy.596
  488.6 10.2 copy.597
  498.8 14.2 scatter_fusion.1
  513.0 52.8 %fusion.695 = (f32[1,8,16,256]{0,3,2,1:T(8,128)}, f32[1,8,16,256]{0,3,2,1:T(8,128)}, f32[1,8,16,256]{0,3,2,1:T(8,128)}, f32[1,8,16,256]{0,3,2,1:T(8,128)}, f32[1,8,16,256]{0,3,2,1:T(8,128)}) fusion(f32[3,9,17,256]{0,3,2,1:T(8,128)} %bitcast.668), kind=kLoop, calls=%fused_computation.913 | loop fusion | bytes 1310720 | tf_op jit(solution)/shard_map/slice | solution.py:72
  616.2 39.2 %all-reduce.19 = (f32[]{:T(128)}, f32[]{:T(128)}) all-reduce(f32[]{:T(128)} %get-tuple-element.8, f32[]{:T(128)} %get-tuple-element.7), channel_id=1, replica_groups=mesh['grp'=16,'sub'=2] {'grp','sub'}, use_global_device_ids=true, to_apply=%region_9.10 | all-reduce | flops 2 | bytes 16 | tf_op jit(solution)/shard_map/psum | solution.py:176
  657.5 40.9 %psum.109 = f32[]{:T(128)} all-reduce(f32[]{:T(128)} %multiply_reduce_fusion.11), channel_id=1, replica_groups=mesh['grp'=16,'sub'=2] {'grp','sub'}, use_global_device_ids=true, to_apply=%region_14.15 | all-reduce | flops 1 | bytes 8 | tf_op jit(solution)/shard_map/psum | solution.py:176
  715.7 10.2 copy.603
  733.4 10.2 copy.604
  743.6 14.3 scatter_fusion.2
  757.9 52.8 %fusion.694 = (f32[1,8,16,256]{0,3,2,1:T(8,128)}, f32[1,8,16,256]{0,3,2,1:T(8,128)}, f32[1,8,16,256]{0,3,2,1:T(8,128)}, f32[1,8,16,256]{0,3,2,1:T(8,128)}, f32[1,8,16,256]{0,3,2,1:T(8,128)}) fusion(f32[3,9,17,256]{0,3,2,1:T(8,128)} %bitcast.669), kind=kLoop, calls=%fused_computation.912 | loop fusion | bytes 1310720 | tf_op jit(solution)/shard_map/slice | solution.py:72
  861.1 40.7 %psum.110 = f32[]{:T(128)} all-reduce(f32[]{:T(128)} %get-tuple-element.27), channel_id=1, replica_groups=mesh['grp'=16,'sub'=2] {'grp','sub'}, use_global_device_ids=true, to_apply=%region_17.18 | all-reduce | flops 1 | bytes 8 | tf_op jit(solution)/shard_map/psum | solution.py:215
  903.8 40.1 %psum.111 = f32[]{:T(128)} all-reduce(f32[]{:T(128)} %get-tuple-element.25), channel_id=1, replica_groups=mesh['grp'=16,'sub'=2] {'grp','sub'}, use_global_device_ids=true, to_apply=%region_19.20 | all-reduce | flops 1 | bytes 8 | tf_op jit(solution)/shard_map/psum | solution.py:176
  962.6 10.2 copy.610
  980.3 10.2 copy.611
  990.5 14.5 scatter_fusion.3
  1005.0 52.8 %fusion.693 = (f32[1,8,16,256]{0,3,2,1:T(8,128)}, f32[1,8,16,256]{0,3,2,1:T(8,128)}, f32[1,8,16,256]{0,3,2,1:T(8,128)}, f32[1,8,16,256]{0,3,2,1:T(8,128)}, f32[1,8,16,256]{0,3,2,1:T(8,128)}) fusion(f32[3,9,17,256]{0,3,2,1:T(8,128)} %bitcast.670), kind=kLoop, calls=%fused_computation.911 | loop fusion | bytes 1310720 | tf_op jit(solution)/shard_map/slice | solution.py:72
  1108.2 40.4 %psum.112 = f32[]{:T(128)} all-reduce(f32[]{:T(128)} %get-tuple-element.23), channel_id=1, replica_groups=mesh['grp'=16,'sub'=2] {'grp','sub'}, use_global_device_ids=true, to_apply=%region_22.23 | all-reduce | flops 1 | bytes 8 | tf_op jit(solution)/shard_map/psum | solution.py:215
  1150.6 40.2 %psum.113 = f32[]{:T(128)} all-reduce(f32[]{:T(128)} %get-tuple-element.21), channel_id=1, replica_groups=mesh['grp'=16,'sub'=2] {'grp','sub'}, use_global_device_ids=true, to_apply=%region_24.25 | all-reduce | flops 1 | bytes 8 | tf_op jit(solution)/shard_map/psum | solution.py:176
  1208.7 10.2 copy.617
  1226.4 10.2 copy.618
  1236.6 14.2 scatter_fusion.4
  1250.8 52.8 %fusion.692 = (f32[1,8,16,256]{0,3,2,1:T(8,128)}, f32[1,8,16,256]{0,3,2,1:T(8,128)}, f32[1,8,16,256]{0,3,2,1:T(8,128)}, f32[1,8,16,256]{0,3,2,1:T(8,128)}, f32[1,8,16,256]{0,3,2,1:T(8,128)}) fusion(f32[3,9,17,256]{0,3,2,1:T(8,128)} %bitcast.671), kind=kLoop, calls=%fused_computation.910 | loop fusion | bytes 1310720 | tf_op jit(solution)/shard_map/slice | solution.py:72
  1354.0 40.7 %psum.114 = f32[]{:T(128)} all-reduce(f32[]{:T(128)} %get-tuple-element.19), channel_id=1, replica_groups=mesh['grp'=16,'sub'=2] {'grp','sub'}, use_global_device_ids=true, to_apply=%region_27.28 | all-reduce | flops 1 | bytes 8 | tf_op jit(solution)/shard_map/psum | solution.py:215
  1396.8 39.9 %psum.115 = f32[]{:T(128)} all-reduce(f32[]{:T(128)} %get-tuple-element.17), channel_id=1, replica_groups=mesh['grp'=16,'sub'=2] {'grp','sub'}, use_global_device_ids=true, to_apply=%region_29.30 | all-reduce | flops 1 | bytes 8 | tf_op jit(solution)/shard_map/psum | solution.py:176
  1455.5 10.2 copy.624
  1473.3 10.2 copy.625
  1483.5 14.2 scatter_fusion.5
  1497.7 52.8 %fusion.691 = (f32[1,8,16,256]{0,3,2,1:T(8,128)}, f32[1,8,16,256]{0,3,2,1:T(8,128)}, f32[1,8,16,256]{0,3,2,1:T(8,128)}, f32[1,8,16,256]{0,3,2,1:T(8,128)}, f32[1,8,16,256]{0,3,2,1:T(8,128)}) fusion(f32[3,9,17,256]{0,3,2,1:T(8,128)} %bitcast.672), kind=kLoop, calls=%fused_computation.909 | loop fusion | bytes 1310720 | tf_op jit(solution)/shard_map/slice | solution.py:72
  1600.9 40.4 %psum.116 = f32[]{:T(128)} all-reduce(f32[]{:T(128)} %get-tuple-element.15), channel_id=1, replica_groups=mesh['grp'=16,'sub'=2] {'grp','sub'}, use_global_device_ids=true, to_apply=%region_32.33 | all-reduce | flops 1 | bytes 8 | tf_op jit(solution)/shard_map/psum | solution.py:215
  1643.3 40.2 %psum.117 = f32[]{:T(128)} all-reduce(f32[]{:T(128)} %get-tuple-element.13), channel_id=1, replica_groups=mesh['grp'=16,'sub'=2] {'grp','sub'}, use_global_device_ids=true, to_apply=%region_34.35 | all-reduce | flops 1 | bytes 8 | tf_op jit(solution)/shard_map/psum | solution.py:176
  1701.5 10.2 copy.631
  1719.2 10.2 copy.632
  1729.4 14.3 scatter_fusion.6
  1743.7 52.8 %fusion.690 = (f32[1,8,16,256]{0,3,2,1:T(8,128)}, f32[1,8,16,256]{0,3,2,1:T(8,128)}, f32[1,8,16,256]{0,3,2,1:T(8,128)}, f32[1,8,16,256]{0,3,2,1:T(8,128)}, f32[1,8,16,256]{0,3,2,1:T(8,128)}) fusion(f32[3,9,17,256]{0,3,2,1:T(8,128)} %bitcast.667), kind=kLoop, calls=%fused_computation.908 | loop fusion | bytes 1310720 | tf_op jit(solution)/shard_map/slice | solution.py:72
  1826.4 10.0 copy.822
  1847.0 40.6 %psum.118 = f32[]{:T(128)} all-reduce(f32[]{:T(128)} %get-tuple-element.11), channel_id=1, replica_groups=mesh['grp'=16,'sub'=2] {'grp','sub'}, use_global_device_ids=true, to_apply=%region_37.38 | all-reduce | flops 1 | bytes 8 | tf_op jit(solution)/shard_map/psum | solution.py:215
  1906.2 10.2 copy.638
  1923.7 41.3 %psum.119 = f32[16,3]{1,0:T(8,128)S(1)} all-reduce(f32[16,3]{1,0:T(8,128)S(1)} %broadcast_select_fusion), channel_id=1, replica_groups=mesh['grp'=16,'sub'=2] {'grp','sub'}, use_global_device_ids=true, to_apply=%region_38.39 | all-reduce | flops 48 | bytes 384 | tf_op jit(solution)/shard_map/psum | solution.py:61
  (616 shorter events, 728.3 us)
Async XLA Ops:
  0.7 83.2 %collective-permute-start.4 = (f32[3,1,1024]{2,1,0:T(1,128)S(1)}, f32[3,1,1024]{2,1,0:T(1,128)S(1)}, u32[]{:S(2)}, u32[]{:S(2)}) collective-permute-start(f32[3,1,1024]{2,1,0:T(1,128)S(1)} %slice.710), channel_id=1, source_target_pairs={{0,1},{1,0},{2,3},{3,2},{4,5},{5,4},{6,7},{7,6},{8,9},{9,8},{10,11... | collective-permute-start | bytes 36872 | tf_op jit(solution)/shard_map/ppermute | solution.py:38
  4.4 9.9 collective-permute-start.1
  5.7 7.7 collective-permute-start
  14.4 6.0 collective-permute-start.3
  15.7 5.9 collective-permute-start.2
  84.6 4.0 collective-permute-start.5
  96.1 9.8 all-to-all-start
  124.9 3.8 collective-permute-start.6
  130.3 9.9 collective-permute-start.7
  178.7 3.8 collective-permute-start.8
  184.8 9.8 collective-permute-start.9
  235.1 3.8 collective-permute-start.10
  241.2 9.9 collective-permute-start.11
  262.3 10.9 all-to-all-start.6
  278.0 9.7 all-to-all-start.7
  294.9 3.8 collective-permute-start.12
  454.9 448.2 %copy-start = (f32[8,16,256]{2,1,0:T(8,128)}, f32[8,16,256]{2,1,0:T(8,128)S(1)}, u32[]{:S(2)}) copy-start(f32[8,16,256]{2,1,0:T(8,128)S(1)} %fusion.102) | copy-start | bytes 393220
  454.9 3.6 collective-permute-start.13
  457.1 3.1 collective-permute-start.14
  460.2 5.3 collective-permute-start.15
  464.2 5.6 collective-permute-start.16
  699.7 245.4 %copy-start.4 = (f32[8,16,256]{2,1,0:T(8,128)}, f32[8,16,256]{2,1,0:T(8,128)S(1)}, u32[]{:S(2)}) copy-start(f32[8,16,256]{2,1,0:T(8,128)S(1)} %multiply_add_fusion.5) | copy-start | bytes 393220
  699.8 2.6 collective-permute-start.17
  701.1 5.8 collective-permute-start.18
  706.9 3.5 collective-permute-start.19
  709.0 5.6 collective-permute-start.20
  945.2 246.9 %copy-start.6 = (f32[8,16,256]{2,1,0:T(8,128)}, f32[8,16,256]{2,1,0:T(8,128)S(1)}, u32[]{:S(2)}) copy-start(f32[8,16,256]{2,1,0:T(8,128)S(1)} %multiply_add_fusion.4) | copy-start | bytes 393220
  945.2 2.6 collective-permute-start.21
  946.5 5.8 collective-permute-start.22
  952.3 4.9 collective-permute-start.23
  955.9 5.6 collective-permute-start.24
  1192.1 245.9 %copy-start.8 = (f32[8,16,256]{2,1,0:T(8,128)}, f32[8,16,256]{2,1,0:T(8,128)S(1)}, u32[]{:S(2)}) copy-start(f32[8,16,256]{2,1,0:T(8,128)S(1)} %multiply_add_fusion.3) | copy-start | bytes 393220
  1192.1 2.6 collective-permute-start.25
  1193.4 5.8 collective-permute-start.26
  1199.2 4.2 collective-permute-start.27
  1202.0 5.6 collective-permute-start.28
  1438.0 2.6 collective-permute-start.29
  1439.3 5.8 collective-permute-start.30
  1445.1 5.1 collective-permute-start.31
  1448.9 5.6 collective-permute-start.32
  1684.9 2.6 collective-permute-start.33
  1686.1 5.8 collective-permute-start.34
  1691.9 4.3 collective-permute-start.35
  1694.8 5.6 collective-permute-start.36
  1889.1 2.6 collective-permute-start.37
  1890.4 5.8 collective-permute-start.38
  1896.2 4.7 collective-permute-start.39
  1899.7 5.6 collective-permute-start.40
  (32 other events, 1661.5 us)
